TPU v7x, 32 devices: a whole 2x2x4 slice. The times are simulated.
32 devices in a mesh: tm: 4 (over y, core), height: 4 (over z), width: 2 (over x).
Axes of the slice: x: 2, y: 2, z: 4, core: 2. Of those that a mesh axis runs over, the one named last changes fastest.
Arguments:
- tokens: bfloat16 [2048, 3072], P(('tm', 'height', 'width'))
- shift_mod: float32 [3072], replicated, may hold values from -3 to 3
- scale_mod: float32 [3072], replicated, may hold values from -2.5 to 2.5
- proj_weight: bfloat16 [64, 3072], replicated, may hold values from -0.109375 to 0.109375
- proj_bias: float32 [64], replicated, may hold values from -3 to 3
- conv1_weight: bfloat16 [3, 3, 3, 16, 512], replicated, may hold values from -0.3125 to 0.3125
- conv1_bias: float32 [512], replicated, may hold values from -3 to 3
- norm_gain: float32 [512], replicated, may hold values from 0.25 to 1.75
- norm_bias: float32 [512], replicated, may hold values from -3 to 3
- conv2_weight: bfloat16 [3, 3, 3, 512, 512], P(None, None, None, 'width'), may hold values from -0.0546875 to 0.0546875
- conv2_bias: float32 [512], replicated, may hold values from -3 to 3
Outputs:
- pixels: bfloat16 [16, 32, 16, 512], P('tm', 'height', 'width')
All inputs are finite; a program needn't handle non-finite values.
Results may differ from a plain program's by a relative error of at most 0.0095.
Values may be sent and summed in bfloat16 or wider, within the bound.
No kernel may reach another device: no remote copies, remote signals or barrier semaphores. Data moves between devices by JAX's collectives and lax.ppermute only.
A program may use at most 128 MiB of HBM per device.

v0:
```python
import jax
import jax.numpy as jnp
from jax import lax
from jax.sharding import PartitionSpec as P

LAT = 16
C1 = 512
GROUPS = 32
FT = 4
TH = 8
TW = 8
PF = 64


def with_halo(x, sides, width):
    for axis, dim in sides:
        peers, length = (lax.axis_size(axis), x.shape[dim])
        up = [(i, (i + 1) % peers) for i in range(peers - 1)]
        down = [(j, i) for i, j in up]
        last = lax.slice_in_dim(x, length - width, length, axis=dim)
        leading = lax.slice_in_dim(x, 0, width, axis=dim)
        before = lax.ppermute(last, axis, up)
        after = lax.ppermute(leading, axis, down)
        x = jnp.concatenate([before, x, after], axis=dim)
    return x


def shifted(value, axis, steps):
    count = lax.axis_size(axis)
    leading, last = (max(0, -steps), min(count, count - steps))
    return lax.ppermute(value, axis, [(source, source + steps) for source in range(leading, last)])


def project(values_in, shift_mod, scale_mod, proj_weight, proj_bias):
    values = values_in.astype(jnp.float32)
    center = jnp.mean(values, axis=-1, keepdims=True)
    spread = jnp.mean((values - center) * (values - center), axis=-1, keepdims=True)
    normed = ((values - center) * lax.rsqrt(spread + 1e-06) * (1.0 + scale_mod) + shift_mod).astype(
        jnp.bfloat16
    )
    projected = lax.dot_general(
        normed, proj_weight, (((1,), (1,)), ((), ())), preferred_element_type=jnp.float32
    )
    result = (projected + proj_bias).astype(jnp.bfloat16)
    return result


def convolve(padded, weight, frames, rows, cols):
    channels = weight.shape[3]
    outputs = weight.shape[4]
    total = jnp.zeros((frames * rows * cols, outputs), jnp.float32)
    for row_tap in range(3):
        for col_tap in range(3):
            window = jnp.concatenate(
                [
                    padded[
                        frame_tap : frame_tap + frames,
                        row_tap : row_tap + rows,
                        col_tap : col_tap + cols,
                        :,
                    ]
                    for frame_tap in range(3)
                ],
                axis=-1,
            )
            taps = weight[:, row_tap, col_tap].reshape(3 * channels, outputs)
            total = total + jnp.dot(
                window.reshape(-1, 3 * channels), taps, preferred_element_type=jnp.float32
            )
    return total.reshape(frames, rows, cols, outputs)


def per_device(
    tokens,
    shift_mod,
    scale_mod,
    proj_weight,
    proj_bias,
    conv1_weight,
    conv1_bias,
    norm_gain,
    norm_bias,
    conv2_weight,
    conv2_bias,
):
    width_count = lax.axis_size("width")
    height_count = lax.axis_size("height")
    time_count = lax.axis_size("tm")
    line_rows = FT * TH // (2 * width_count)
    half_rows = TH // 2
    half_cols = TW // 2
    local_patches = project(tokens, shift_mod, scale_mod, proj_weight, proj_bias)
    sectioned = local_patches.reshape(line_rows, width_count, half_cols, PF)
    sectioned = lax.all_to_all(sectioned, "width", split_axis=1, concat_axis=0, tiled=True)
    sectioned = sectioned.reshape(FT // height_count, height_count, half_rows, half_cols, PF)
    sectioned = lax.all_to_all(sectioned, "height", split_axis=1, concat_axis=0, tiled=True)
    patches = sectioned.reshape(FT, half_rows, half_cols, PF)
    latent = (
        patches.reshape(FT, half_rows, half_cols, LAT, 2, 2)
        .transpose(0, 1, 4, 2, 5, 3)
        .reshape(FT, TH, TW, LAT)
    )
    group_size = C1 // GROUPS
    count = FT * TH * TW * time_count * height_count * width_count * group_size
    padded = with_halo(latent, (("height", 1), ("width", 2)), 2)
    earlier = shifted(padded, "tm", 1)
    stacked = jnp.concatenate([earlier, padded], axis=0)
    hidden = (convolve(stacked, conv1_weight, FT + 2, TH + 2, TW + 2) + conv1_bias).astype(
        jnp.bfloat16
    )
    grouped = hidden[2:, 1:-1, 1:-1].astype(jnp.float32).reshape(-1, GROUPS, group_size)
    sums = jnp.sum(grouped, axis=(0, 2))
    squares = jnp.sum(grouped * grouped, axis=(0, 2))
    sums, squares = lax.psum((sums, squares), ("tm", "height", "width"))
    gmean = sums / count
    gvar = squares / count - gmean * gmean
    mean_full = jnp.repeat(gmean, group_size)
    inverse_full = jnp.repeat(lax.rsqrt(gvar + 1e-06), group_size)
    scaled = (hidden.astype(jnp.float32) - mean_full) * inverse_full * norm_gain + norm_bias
    activated = jax.nn.silu(scaled).astype(jnp.bfloat16)
    frame_global = lax.axis_index("tm") * FT - 2 + jnp.arange(FT + 2)
    row_global = lax.axis_index("height") * TH - 1 + jnp.arange(TH + 2)
    col_global = lax.axis_index("width") * TW - 1 + jnp.arange(TW + 2)
    frame_valid = frame_global >= 0
    row_valid = (row_global >= 0) & (row_global < TH * height_count)
    col_valid = (col_global >= 0) & (col_global < TW * width_count)
    inside = (
        frame_valid[:, None, None, None]
        & row_valid[None, :, None, None]
        & col_valid[None, None, :, None]
    )
    act_stacked = jnp.where(inside, activated, jnp.zeros_like(activated))
    total = convolve(
        act_stacked, lax.all_gather(conv2_weight, "width", axis=3, tiled=True), FT, TH, TW
    )
    return (total + conv2_bias).astype(jnp.bfloat16)


def solution(mesh):
    placed = (
        P(("tm", "height", "width"), None),
        P(),
        P(),
        P(),
        P(),
        P(),
        P(),
        P(),
        P(),
        P(None, None, None, "width", None),
        P(),
    )
    return jax.shard_map(
        per_device,
        mesh=mesh,
        in_specs=placed,
        out_specs=P("tm", "height", "width", None),
        check_vma=False,
    )
```

profile of v0, /device:TPU:0, one launch (start us, length us, event | category | flops | bytes accessed | tf_op | source)
XLA Modules:
  0.0 205.0 jit_solution(6254833569561330727)
XLA Ops:
  9.1 4.2 %all-to-all-start = ((bf16[2,2,1024]{2,1,0:T(2,128)(2,1)}), bf16[2,2,1024]{2,1,0:T(2,128)(2,1)S(1)}, u32[]{:S(2)}, u32[]{:S(2)}) async-start(bf16[2,2,1024]{2,1,0:T(2,128)(2,1)} %reshape.178), calls=%async_computation | async-start | bytes 16384 | tf_op jit(solution)/shard_map/all_to_all | solution.py:94
  13.4 0.8 fusion.17
  14.1 3.1 %all-to-all-done = bf16[2,2,1024]{2,1,0:T(2,128)(2,1)S(1)} async-done(((bf16[2,2,1024]{2,1,0:T(2,128)(2,1)}), bf16[2,2,1024]{2,1,0:T(2,128)(2,1)S(1)}, u32[]{:S(2)}, u32[]{:S(2)}) %all-to-all-start) | async-done | bytes 8224 | tf_op jit(solution)/shard_map/all_to_all | solution.py:94
  18.0 5.3 %all-to-all-start.1 = ((bf16[4,2,512]{2,1,0:T(2,128)(2,1)}), bf16[4,2,512]{2,1,0:T(2,128)(2,1)S(1)}, u32[]{:S(2)}, u32[]{:S(2)}) async-start(bf16[4,2,512]{2,1,0:T(2,128)(2,1)} %reshape.180), calls=%async_computation.1 | async-start | bytes 16384 | tf_op jit(solution)/shard_map/all_to_all | solution.py:96
  23.3 5.6 %all-to-all-done.1 = bf16[4,2,512]{2,1,0:T(2,128)(2,1)S(1)} async-done(((bf16[4,2,512]{2,1,0:T(2,128)(2,1)}), bf16[4,2,512]{2,1,0:T(2,128)(2,1)S(1)}, u32[]{:S(2)}, u32[]{:S(2)}) %all-to-all-start.1) | async-done | bytes 8224 | tf_op jit(solution)/shard_map/all_to_all | solution.py:96
  29.7 2.5 %collective-permute-start = (bf16[4,2,8,16]{3,2,1,0:T(8,128)(2,1)S(1)}, bf16[4,2,8,16]{3,2,1,0:T(8,128)(2,1)S(1)}, u32[]{:S(2)}, u32[]{:S(2)}) collective-permute-start(bf16[4,2,8,16]{3,2,1,0:T(8,128)(2,1)S(1)} %get-tuple-element.83), channel_id=1, source_target_pairs={{0,2},{2,4},{4,6},{1,3},{3,5},{5,7},{8,10},{10,12},{12,14},{9,11},... | collective-permute-start | bytes 6152 | tf_op jit(solution)/shard_map/ppermute | solution.py:22
  32.2 1.3 collective-permute-start.1
  33.7 4.2 %collective-permute-done.1 = bf16[4,2,8,16]{3,2,1,0:T(8,128)(2,1)S(1)} collective-permute-done((bf16[4,2,8,16]{3,2,1,0:T(8,128)(2,1)S(1)}, bf16[4,2,8,16]{3,2,1,0:T(8,128)(2,1)S(1)}, u32[]{:S(2)}, u32[]{:S(2)}) %collective-permute-start.1) | collective-permute-done | bytes 2080 | tf_op jit(solution)/shard_map/ppermute | solution.py:23
  37.9 1.9 collective-permute-start.2
  39.8 1.3 collective-permute-start.3
  41.8 4.4 %collective-permute-done.3 = bf16[4,12,2,16]{3,2,1,0:T(2,128)(2,1)S(1)} collective-permute-done((bf16[4,12,2,16]{3,2,1,0:T(2,128)(2,1)S(1)}, bf16[4,12,2,16]{3,2,1,0:T(2,128)(2,1)S(1)}, u32[]{:S(2)}, u32[]{:S(2)}) %collective-permute-start.3) | collective-permute-done | bytes 3104 | tf_op jit(solution)/shard_map/ppermute | solution.py:23
  46.3 1.3 collective-permute-start.4
  47.7 1.0 collective-permute-done.4
  48.8 1.1 fusion.19
  51.9 1.6 fusion.18
  53.8 2.7 %pad_maximum_fusion.11 = (bf16[6,10,10,48]{3,2,1,0:T(8,128)(2,1)}, bf16[6,10,10,48]{3,2,1,0:T(8,128)(2,1)S(1)}) fusion(bf16[6,10,10,16]{3,2,1,0:T(8,128)(2,1)} %get-tuple-element.72, bf16[6,10,10,16]{3,2,1,0:T(8,128)(2,1)} %get-tuple-element.74, bf16[6,10,10,16]{3,2,1,0:T(8,128)(2,1)} %get-tuple-element.73, bf16[6,10,10,16]{3,2,1,0:T(8,128)(2,1)} %get-tuple-element.69, ...), kind=kLoop, calls=%fused_computation.49 | loop fusion | flops 345600 | bytes 230400 | tf_op jit(solution)/shard_map/concatenate | solution.py:54
  56.5 1.7 reshape.160
  58.2 0.8 reshape.161
  58.9 1.2 pad_maximum_fusion.15
  60.1 1.0 reshape.164
  66.4 1.3 convolution_add_fusion
  67.7 1.4 reshape.167
  70.1 43.8 %all-reduce = (f32[32]{0:T(128)S(1)}, f32[32]{0:T(128)S(1)}) all-reduce(f32[32]{0:T(128)S(1)} %reduce_sum.57, f32[32]{0:T(128)S(1)} %reduce_sum.54), channel_id=1, replica_groups=mesh['tm'=4,'height'=4,'width'=2] {'tm','height','width'}, use_global_device_ids=true, to_apply=%region_7.8 | all-reduce | flops 64 | bytes 512 | tf_op jit(solution)/shard_map/psum | solution.py:114
  114.2 0.8 fusion.1
  115.4 0.8 fusion.15
  116.2 1.0 pad_maximum_fusion.2
  117.2 1.0 pad_maximum_fusion.6
  118.2 0.9 pad_maximum_fusion.5
  119.1 1.0 pad_maximum_fusion.4
  120.1 1.0 pad_maximum_fusion.3
  121.1 62.3 %all-gather.2.cloned.1.call-done = bf16[3,3,3,512,512]{4,3,2,1,0:T(8,128)(2,1)} async-done(((bf16[3,3,3,256,512]{4,3,2,1,0:T(8,128)(2,1)}), bf16[3,3,3,512,512]{4,3,2,1,0:T(8,128)(2,1)}) %all-gather.2.cloned.1.call-update) | async-done | bytes 14155792 | tf_op jit(solution)/shard_map/all_gather | solution.py:134
  183.4 5.9 %fusion.14 = (bf16[3,1,1,512,512]{4,3,2,1,0:T(8,128)(2,1)S(1)}, bf16[3,1,1,512,512]{4,3,2,1,0:T(8,128)(2,1)S(1)}, bf16[3,1,1,512,512]{4,3,2,1,0:T(8,128)(2,1)S(1...) fusion(bf16[3,3,3,512,512]{4,3,2,1,0:T(8,128)(2,1)} %all-gather, ...), kind=kLoop, calls=%fused_computation.70 | loop fusion | bytes 28311552 | tf_op jit(solution)/shard_map/slice | solution.py:66
  (125 shorter events, 23.1 us)
Async XLA Ops:
  6.5 1.5 copy-start
  6.5 1.0 copy-start.7
  6.5 1.5 copy-start.20
  6.5 1.5 copy-start.26
  6.5 1.5 copy-start.25
  6.5 176.8 %all-gather.2.cloned.1.call-start = ((), (), s32[]{:S(2)}) async-start(), calls=%async_computation.2 | async-start | bytes 21233664 | tf_op jit(solution)/shard_map/all_gather | solution.py:134
  7.6 5.8 %copy-start.12 = (bf16[3,3,3,16,512]{4,3,2,1,0:T(8,128)(2,1)S(1)}, bf16[3,3,3,16,512]{4,3,2,1,0:T(8,128)(2,1)}, u32[]{:S(2)}) copy-start(bf16[3,3,3,16,512]{4,3,2,1,0:T(8,128)(2,1)} %param.16) | copy-start | bytes 1327108
  9.1 8.1 %all-to-all-start = ((bf16[2,2,1024]{2,1,0:T(2,128)(2,1)}), bf16[2,2,1024]{2,1,0:T(2,128)(2,1)S(1)}, u32[]{:S(2)}, u32[]{:S(2)}) async-start(bf16[2,2,1024]{2,1,0:T(2,128)(2,1)} %reshape.178), calls=%async_computation | async-start | bytes 16384 | tf_op jit(solution)/shard_map/all_to_all | solution.py:94
  18.0 10.9 %all-to-all-start.1 = ((bf16[4,2,512]{2,1,0:T(2,128)(2,1)}), bf16[4,2,512]{2,1,0:T(2,128)(2,1)S(1)}, u32[]{:S(2)}, u32[]{:S(2)}) async-start(bf16[4,2,512]{2,1,0:T(2,128)(2,1)} %reshape.180), calls=%async_computation.1 | async-start | bytes 16384 | tf_op jit(solution)/shard_map/all_to_all | solution.py:96
  29.7 4.0 %collective-permute-start = (bf16[4,2,8,16]{3,2,1,0:T(8,128)(2,1)S(1)}, bf16[4,2,8,16]{3,2,1,0:T(8,128)(2,1)S(1)}, u32[]{:S(2)}, u32[]{:S(2)}) collective-permute-start(bf16[4,2,8,16]{3,2,1,0:T(8,128)(2,1)S(1)} %get-tuple-element.83), channel_id=1, source_target_pairs={{0,2},{2,4},{4,6},{1,3},{3,5},{5,7},{8,10},{10,12},{12,14},{9,11},... | collective-permute-start | bytes 6152 | tf_op jit(solution)/shard_map/ppermute | solution.py:22
  32.2 5.6 %collective-permute-start.1 = (bf16[4,2,8,16]{3,2,1,0:T(8,128)(2,1)S(1)}, bf16[4,2,8,16]{3,2,1,0:T(8,128)(2,1)S(1)}, u32[]{:S(2)}, u32[]{:S(2)}) collective-permute-start(bf16[4,2,8,16]{3,2,1,0:T(8,128)(2,1)S(1)} %get-tuple-element.84), channel_id=1, source_target_pairs={{2,0},{4,2},{6,4},{3,1},{5,3},{7,5},{10,8},{12,10},{14,12},{11,9},... | collective-permute-start | bytes 6152 | tf_op jit(solution)/shard_map/ppermute | solution.py:23
  37.9 3.9 %collective-permute-start.2 = (bf16[4,12,2,16]{3,2,1,0:T(2,128)(2,1)S(1)}, bf16[4,12,2,16]{3,2,1,0:T(2,128)(2,1)S(1)}, u32[]{:S(2)}, u32[]{:S(2)}) collective-permute-start(bf16[4,12,2,16]{3,2,1,0:T(2,128)(2,1)S(1)} %get-tuple-element.81), channel_id=1, source_target_pairs={{0,1},{2,3},{4,5},{6,7},{8,9},{10,11},{12,13},{14,15},{16,17},{18,... | collective-permute-start | bytes 9224 | tf_op jit(solution)/shard_map/ppermute | solution.py:22
  39.8 6.4 %collective-permute-start.3 = (bf16[4,12,2,16]{3,2,1,0:T(2,128)(2,1)S(1)}, bf16[4,12,2,16]{3,2,1,0:T(2,128)(2,1)S(1)}, u32[]{:S(2)}, u32[]{:S(2)}) collective-permute-start(bf16[4,12,2,16]{3,2,1,0:T(2,128)(2,1)S(1)} %get-tuple-element.82), channel_id=1, source_target_pairs={{1,0},{3,2},{5,4},{7,6},{9,8},{11,10},{13,12},{15,14},{17,16},{19,... | collective-permute-start | bytes 9224 | tf_op jit(solution)/shard_map/ppermute | solution.py:23
  46.3 2.4 %collective-permute-start.4 = (bf16[4,12,12,16]{3,2,1,0:T(8,128)(2,1)S(1)}, bf16[4,12,12,16]{3,2,1,0:T(8,128)(2,1)S(1)}, u32[]{:S(2)}, u32[]{:S(2)}) collective-permute-start(bf16[4,12,12,16]{3,2,1,0:T(8,128)(2,1)S(1)} %pad_maximum_fusion.18), channel_id=1, source_target_pairs={{0,8},{8,16},{16,24},{1,9},{9,17},{17,25},{2,10},{10,18},{18,26},{... | collective-permute-start | bytes 55304 | tf_op jit(solution)/shard_map/ppermute | solution.py:31
  61.1 0.9 copy-start.8
  61.7 0.9 copy-start.9
  61.7 0.9 copy-start.19
  62.3 0.9 copy-start.11
  62.3 0.9 copy-start.18
  63.0 0.9 copy-start.10
  63.0 0.9 copy-start.17
  63.6 0.8 copy-start.16
  64.7 0.8 copy-start.14
  67.7 1.4 copy-start.21
  69.1 45.1 %copy-start.22 = (f32[512]{0:T(512)S(1)}, f32[512]{0:T(512)}, u32[]{:S(2)}) copy-start(f32[512]{0:T(512)} %param.19) | copy-start | bytes 6148
  69.1 45.1 %copy-start.23 = (f32[512]{0:T(512)S(1)}, f32[512]{0:T(512)}, u32[]{:S(2)}) copy-start(f32[512]{0:T(512)} %param.18) | copy-start | bytes 6148
  189.9 1.1 copy-start.3
  191.0 1.1 copy-start.6
  192.1 1.1 copy-start.5
  193.3 1.1 copy-start.4
  194.4 1.1 copy-start.2
  196.7 1.5 copy-start.1
  (3 other events, 2.3 us)
Sparse Core Ops, SparseCore 0:
  8.9 174.3 all-gather.1
where the time goes:
time: 206 us; the launch traced here: 205 us
  waiting for transfers between devices  82 us (40%)
  blocking collectives  43.8 us (21%)
  local copies, waits for them, and re-layouts  25 us (12%)
  starting transfers between devices  17.9 us (9%)
  between operations  14 us (7%)
  other arithmetic  13.3 us (6%)
  matrix products  9.1 us (4%)
    all_gather x1, waiting for transfers between devices, per_device(): lax.all_gather(conv2_weight, 'width', axis=3, tiled=True)  62.3 us
    psum x1, blocking collectives, per_device(): sums, squares = lax.psum((sums, squares), ('tm', 'height', 'width'))  43.8 us
    concatenate x14, other arithmetic, convolve(): jnp.concatenate([padded[frame_tap:frame_tap + frames, row_tap:row_tap + r...  10.1 us
    dot_general x18, matrix products, convolve(): jnp.dot(window.reshape(-1, 3 * channels), taps, preferred_element_type=jn...  8.74 us
    ppermute x2, waiting for transfers between devices, with_halo(): after = lax.ppermute(leading, axis, down)  8.6 us
    unnamed x58, local copies, waits for them, and re-layouts  6.88 us
    slice x2, local copies, waits for them, and re-layouts, convolve(): taps = weight[:, row_tap, col_tap].reshape(3 * channels, outputs)  6.68 us
    all_to_all x1, waiting for transfers between devices, per_device(): lax.all_to_all(sectioned, 'height', split_axis=1, concat_axis=0, tiled=True)  5.58 us
  transfers between devices with their start and end apart: 8, of which 8 were waited for; matrix products, arithmetic and copies ran while one was open for 15% of the time, Pallas kernels for 0%

commit v1 on v0

--- a/solution.py
+++ b/solution.py
@@ -131,7 +131,7 @@
     )
     act_stacked = jnp.where(inside, activated, jnp.zeros_like(activated))
     total = convolve(
-        act_stacked, lax.all_gather(conv2_weight, "width", axis=3, tiled=True), FT, TH, TW
+        act_stacked, jnp.concatenate(lax.all_gather(conv2_weight, "width"), axis=3), FT, TH, TW
     )
     return (total + conv2_bias).astype(jnp.bfloat16)
 

time: 206 us -> 212 us (1.029)
  local copies, waits for them, and re-layouts: 25 us -> 29.6 us
  waiting for transfers between devices: 82 us -> 78.3 us
  other arithmetic: 13.3 us -> 16.8 us
    reshape x0 -> x1, local copies, waits for them, and re-layouts: none -> 6.78 us  [per_device(): jnp.concatenate(lax.all_gather(conv2_weight, 'width'), axis=3)]
    all_gather x1, waiting for transfers between devices: 62.3 us -> 58.7 us  [per_device(): lax.all_gather(conv2_weight, 'width')]
    concatenate x14, other arithmetic: 10.1 us -> 13.6 us  [convolve(): jnp.concatenate([padded[frame_tap:frame_tap + frames, row_tap:row_tap + r...]
    slice x2, local copies, waits for them, and re-layouts: 6.68 us -> 3.32 us  [convolve(): taps = weight[:, row_tap, col_tap].reshape(3 * channels, outputs)]
    unnamed x58 -> x64, local copies, waits for them, and re-layouts: 6.88 us -> 7.95 us
  transfers between devices with their start and end apart: 8 -> 8, of which waited for: 8 -> 8; matrix products, arithmetic and copies ran while one was open for 15% -> 16% of each run, Pallas kernels for 0% -> 0%
where the time goes in v1:
time: 212 us; the launch traced here: 211 us
  waiting for transfers between devices  78.3 us (37%)
  blocking collectives  43.8 us (21%)
  local copies, waits for them, and re-layouts  29.6 us (14%)
  starting transfers between devices  17.9 us (8%)
  other arithmetic  16.8 us (8%)
  between operations  13.9 us (7%)
  matrix products  10.8 us (5%)
    all_gather x1, waiting for transfers between devices, per_device(): lax.all_gather(conv2_weight, 'width')  58.7 us
    psum x1, blocking collectives, per_device(): sums, squares = lax.psum((sums, squares), ('tm', 'height', 'width'))  43.8 us
    concatenate x14, other arithmetic, convolve(): jnp.concatenate([padded[frame_tap:frame_tap + frames, row_tap:row_tap + r...  13.6 us
    dot_general x18, matrix products, convolve(): jnp.dot(window.reshape(-1, 3 * channels), taps, preferred_element_type=jn...  10.5 us
    ppermute x2, waiting for transfers between devices, with_halo(): after = lax.ppermute(leading, axis, down)  8.6 us
    unnamed x64, local copies, waits for them, and re-layouts  7.95 us
    reshape x1, local copies, waits for them, and re-layouts, per_device(): jnp.concatenate(lax.all_gather(conv2_weight, 'width'), axis=3)  6.78 us
    all_to_all x1, waiting for transfers between devices, per_device(): lax.all_to_all(sectioned, 'height', split_axis=1, concat_axis=0, tiled=True)  5.58 us
  transfers between devices with their start and end apart: 8, of which 8 were waited for; matrix products, arithmetic and copies ran while one was open for 16% of the time, Pallas kernels for 0%

profile of v1, /device:TPU:0, one launch (start us, length us, event | category | flops | bytes accessed | tf_op | source)
XLA Modules:
  0.0 211.2 jit_solution(11491127193564791336)
XLA Ops:
  9.1 4.2 %all-to-all-start = ((bf16[2,2,1024]{2,1,0:T(2,128)(2,1)}), bf16[2,2,1024]{2,1,0:T(2,128)(2,1)S(1)}, u32[]{:S(2)}, u32[]{:S(2)}) async-start(bf16[2,2,1024]{2,1,0:T(2,128)(2,1)} %reshape.187), calls=%async_computation | async-start | bytes 16384 | tf_op jit(solution)/shard_map/all_to_all | solution.py:94
  14.1 3.1 %all-to-all-done = bf16[2,2,1024]{2,1,0:T(2,128)(2,1)S(1)} async-done(((bf16[2,2,1024]{2,1,0:T(2,128)(2,1)}), bf16[2,2,1024]{2,1,0:T(2,128)(2,1)S(1)}, u32[]{:S(2)}, u32[]{:S(2)}) %all-to-all-start) | async-done | bytes 8224 | tf_op jit(solution)/shard_map/all_to_all | solution.py:94
  18.0 5.3 %all-to-all-start.1 = ((bf16[4,2,512]{2,1,0:T(2,128)(2,1)}), bf16[4,2,512]{2,1,0:T(2,128)(2,1)S(1)}, u32[]{:S(2)}, u32[]{:S(2)}) async-start(bf16[4,2,512]{2,1,0:T(2,128)(2,1)} %reshape.189), calls=%async_computation.1 | async-start | bytes 16384 | tf_op jit(solution)/shard_map/all_to_all | solution.py:96
  23.3 5.6 %all-to-all-done.1 = bf16[4,2,512]{2,1,0:T(2,128)(2,1)S(1)} async-done(((bf16[4,2,512]{2,1,0:T(2,128)(2,1)}), bf16[4,2,512]{2,1,0:T(2,128)(2,1)S(1)}, u32[]{:S(2)}, u32[]{:S(2)}) %all-to-all-start.1) | async-done | bytes 8224 | tf_op jit(solution)/shard_map/all_to_all | solution.py:96
  29.7 2.5 %collective-permute-start = (bf16[4,2,8,16]{3,2,1,0:T(8,128)(2,1)S(1)}, bf16[4,2,8,16]{3,2,1,0:T(8,128)(2,1)S(1)}, u32[]{:S(2)}, u32[]{:S(2)}) collective-permute-start(bf16[4,2,8,16]{3,2,1,0:T(8,128)(2,1)S(1)} %get-tuple-element.83), channel_id=1, source_target_pairs={{0,2},{2,4},{4,6},{1,3},{3,5},{5,7},{8,10},{10,12},{12,14},{9,11},... | collective-permute-start | bytes 6152 | tf_op jit(solution)/shard_map/ppermute | solution.py:22
  32.2 1.3 collective-permute-start.1
  33.7 4.2 %collective-permute-done.1 = bf16[4,2,8,16]{3,2,1,0:T(8,128)(2,1)S(1)} collective-permute-done((bf16[4,2,8,16]{3,2,1,0:T(8,128)(2,1)S(1)}, bf16[4,2,8,16]{3,2,1,0:T(8,128)(2,1)S(1)}, u32[]{:S(2)}, u32[]{:S(2)}) %collective-permute-start.1) | collective-permute-done | bytes 2080 | tf_op jit(solution)/shard_map/ppermute | solution.py:23
  37.9 1.9 collective-permute-start.2
  39.8 1.3 collective-permute-start.3
  41.8 4.4 %collective-permute-done.3 = bf16[4,12,2,16]{3,2,1,0:T(2,128)(2,1)S(1)} collective-permute-done((bf16[4,12,2,16]{3,2,1,0:T(2,128)(2,1)S(1)}, bf16[4,12,2,16]{3,2,1,0:T(2,128)(2,1)S(1)}, u32[]{:S(2)}, u32[]{:S(2)}) %collective-permute-start.3) | collective-permute-done | bytes 3104 | tf_op jit(solution)/shard_map/ppermute | solution.py:23
  46.3 1.3 collective-permute-start.4
  47.7 1.0 collective-permute-done.4
  48.9 1.1 fusion.19
  51.9 1.6 fusion.18
  53.9 2.7 %pad_maximum_fusion.11 = (bf16[6,10,10,48]{3,2,1,0:T(8,128)(2,1)}, bf16[6,10,10,48]{3,2,1,0:T(8,128)(2,1)S(1)}) fusion(bf16[6,10,10,16]{3,2,1,0:T(8,128)(2,1)} %get-tuple-element.72, bf16[6,10,10,16]{3,2,1,0:T(8,128)(2,1)} %get-tuple-element.74, bf16[6,10,10,16]{3,2,1,0:T(8,128)(2,1)} %get-tuple-element.73, bf16[6,10,10,16]{3,2,1,0:T(8,128)(2,1)} %get-tuple-element.69, ...), kind=kLoop, calls=%fused_computation.49 | loop fusion | flops 345600 | bytes 230400 | tf_op jit(solution)/shard_map/concatenate | solution.py:54
  56.5 1.7 reshape.166
  59.0 1.2 pad_maximum_fusion.15
  60.1 1.0 reshape.170
  66.4 1.3 convolution_add_fusion
  67.8 1.4 reshape.173
  70.1 43.8 %all-reduce = (f32[32]{0:T(128)S(1)}, f32[32]{0:T(128)S(1)}) all-reduce(f32[32]{0:T(128)S(1)} %reduce_sum.57, f32[32]{0:T(128)S(1)} %reduce_sum.54), channel_id=1, replica_groups=mesh['tm'=4,'height'=4,'width'=2] {'tm','height','width'}, use_global_device_ids=true, to_apply=%region_7.8 | all-reduce | flops 64 | bytes 512 | tf_op jit(solution)/shard_map/psum | solution.py:114
  115.4 1.0 pad_maximum_fusion.1
  116.3 0.9 pad_maximum_fusion
  118.0 1.0 pad_maximum_fusion.8
  119.0 1.0 pad_maximum_fusion.2
  120.0 0.9 pad_maximum_fusion.7
  122.8 1.0 pad_maximum_fusion.4
  123.8 0.9 pad_maximum_fusion.3
  124.7 58.7 %all-gather.3.cloned.1.call-done = bf16[6,3,3,256,512]{4,3,2,1,0:T(8,128)(2,1)} async-done(((bf16[3,3,3,256,512]{4,3,2,1,0:T(8,128)(2,1)}), bf16[6,3,3,256,512]{4,3,2,1,0:T(8,128)(2,1)}) %all-gather.3.cloned.1.call-update) | async-done | bytes 14155792 | tf_op jit(solution)/shard_map/all_gather | solution.py:134
  183.4 6.8 %copy.24 = bf16[3,3,3,2,256,512]{5,4,3,2,1,0:T(8,128)(2,1)S(1)} copy(bf16[3,3,3,2,256,512]{5,4,2,1,0,3:T(8,128)(2,1)} %bitcast.88) | data formatting | bytes 28311552 | tf_op jit(solution)/shard_map/reshape | solution.py:134
  190.1 2.6 %fusion.14 = (bf16[3,1,1,512,512]{4,3,2,1,0:T(8,128)(2,1)S(1)}, bf16[3,1,1,512,512]{4,3,2,1,0:T(8,128)(2,1)S(1)}, bf16[3,1,1,512,512]{4,3,2,1,0:T(8,128)(2,1)S(1...) fusion(bf16[3,3,3,512,512]{4,3,2,1,0:T(8,128)(2,1)S(1)} %bitcast.87), kind=kLoop, calls=%fused_computation.70 | loop fusion | bytes 28311552 | tf_op jit(solution)/shard_map/slice | solution.py:66
  192.7 2.3 %fusion.22 = f32[256,512]{1,0:T(8,128)S(1)} fusion(bf16[256,1536]{1,0:T(8,128)(2,1)} %bitcast.98, bf16[1536,512]{1,0:T(8,128)(2,1)} %bitcast.97), kind=kOutput, calls=%fused_computation.80 | convolution fusion | flops 402653184 | bytes 2883584 | tf_op jit(solution)/shard_map/dot_general | solution.py:67
  (132 shorter events, 28.4 us)
Async XLA Ops:
  6.5 1.5 copy-start
  6.5 1.0 copy-start.10
  6.5 1.5 copy-start.23
  6.5 1.5 copy-start.29
  6.5 1.5 copy-start.28
  6.5 176.8 %all-gather.3.cloned.1.call-start = ((), (), s32[]{:S(2)}) async-start(), calls=%async_computation.2 | async-start | bytes 21233664 | tf_op jit(solution)/shard_map/all_gather | solution.py:134
  7.6 5.8 %copy-start.15 = (bf16[3,3,3,16,512]{4,3,2,1,0:T(8,128)(2,1)S(1)}, bf16[3,3,3,16,512]{4,3,2,1,0:T(8,128)(2,1)}, u32[]{:S(2)}) copy-start(bf16[3,3,3,16,512]{4,3,2,1,0:T(8,128)(2,1)} %param.16) | copy-start | bytes 1327108
  9.1 8.1 %all-to-all-start = ((bf16[2,2,1024]{2,1,0:T(2,128)(2,1)}), bf16[2,2,1024]{2,1,0:T(2,128)(2,1)S(1)}, u32[]{:S(2)}, u32[]{:S(2)}) async-start(bf16[2,2,1024]{2,1,0:T(2,128)(2,1)} %reshape.187), calls=%async_computation | async-start | bytes 16384 | tf_op jit(solution)/shard_map/all_to_all | solution.py:94
  18.0 10.9 %all-to-all-start.1 = ((bf16[4,2,512]{2,1,0:T(2,128)(2,1)}), bf16[4,2,512]{2,1,0:T(2,128)(2,1)S(1)}, u32[]{:S(2)}, u32[]{:S(2)}) async-start(bf16[4,2,512]{2,1,0:T(2,128)(2,1)} %reshape.189), calls=%async_computation.1 | async-start | bytes 16384 | tf_op jit(solution)/shard_map/all_to_all | solution.py:96
  29.7 4.0 %collective-permute-start = (bf16[4,2,8,16]{3,2,1,0:T(8,128)(2,1)S(1)}, bf16[4,2,8,16]{3,2,1,0:T(8,128)(2,1)S(1)}, u32[]{:S(2)}, u32[]{:S(2)}) collective-permute-start(bf16[4,2,8,16]{3,2,1,0:T(8,128)(2,1)S(1)} %get-tuple-element.83), channel_id=1, source_target_pairs={{0,2},{2,4},{4,6},{1,3},{3,5},{5,7},{8,10},{10,12},{12,14},{9,11},... | collective-permute-start | bytes 6152 | tf_op jit(solution)/shard_map/ppermute | solution.py:22
  32.2 5.6 %collective-permute-start.1 = (bf16[4,2,8,16]{3,2,1,0:T(8,128)(2,1)S(1)}, bf16[4,2,8,16]{3,2,1,0:T(8,128)(2,1)S(1)}, u32[]{:S(2)}, u32[]{:S(2)}) collective-permute-start(bf16[4,2,8,16]{3,2,1,0:T(8,128)(2,1)S(1)} %get-tuple-element.84), channel_id=1, source_target_pairs={{2,0},{4,2},{6,4},{3,1},{5,3},{7,5},{10,8},{12,10},{14,12},{11,9},... | collective-permute-start | bytes 6152 | tf_op jit(solution)/shard_map/ppermute | solution.py:23
  37.9 3.9 %collective-permute-start.2 = (bf16[4,12,2,16]{3,2,1,0:T(2,128)(2,1)S(1)}, bf16[4,12,2,16]{3,2,1,0:T(2,128)(2,1)S(1)}, u32[]{:S(2)}, u32[]{:S(2)}) collective-permute-start(bf16[4,12,2,16]{3,2,1,0:T(2,128)(2,1)S(1)} %get-tuple-element.81), channel_id=1, source_target_pairs={{0,1},{2,3},{4,5},{6,7},{8,9},{10,11},{12,13},{14,15},{16,17},{18,... | collective-permute-start | bytes 9224 | tf_op jit(solution)/shard_map/ppermute | solution.py:22
  39.8 6.4 %collective-permute-start.3 = (bf16[4,12,2,16]{3,2,1,0:T(2,128)(2,1)S(1)}, bf16[4,12,2,16]{3,2,1,0:T(2,128)(2,1)S(1)}, u32[]{:S(2)}, u32[]{:S(2)}) collective-permute-start(bf16[4,12,2,16]{3,2,1,0:T(2,128)(2,1)S(1)} %get-tuple-element.82), channel_id=1, source_target_pairs={{1,0},{3,2},{5,4},{7,6},{9,8},{11,10},{13,12},{15,14},{17,16},{19,... | collective-permute-start | bytes 9224 | tf_op jit(solution)/shard_map/ppermute | solution.py:23
  46.3 2.4 %collective-permute-start.4 = (bf16[4,12,12,16]{3,2,1,0:T(8,128)(2,1)S(1)}, bf16[4,12,12,16]{3,2,1,0:T(8,128)(2,1)S(1)}, u32[]{:S(2)}, u32[]{:S(2)}) collective-permute-start(bf16[4,12,12,16]{3,2,1,0:T(8,128)(2,1)S(1)} %pad_maximum_fusion.18), channel_id=1, source_target_pairs={{0,8},{8,16},{16,24},{1,9},{9,17},{17,25},{2,10},{10,18},{18,26},{... | collective-permute-start | bytes 55304 | tf_op jit(solution)/shard_map/ppermute | solution.py:31
  61.8 0.9 copy-start.12
  61.8 0.9 copy-start.22
  62.4 0.9 copy-start.14
  62.4 0.9 copy-start.21
  63.0 0.9 copy-start.13
  63.0 0.9 copy-start.20
  67.8 1.4 copy-start.24
  69.2 45.1 %copy-start.25 = (f32[512]{0:T(512)S(1)}, f32[512]{0:T(512)}, u32[]{:S(2)}) copy-start(f32[512]{0:T(512)} %param.19) | copy-start | bytes 6148
  69.2 45.1 %copy-start.26 = (f32[512]{0:T(512)S(1)}, f32[512]{0:T(512)}, u32[]{:S(2)}) copy-start(f32[512]{0:T(512)} %param.18) | copy-start | bytes 6148
  192.7 2.3 %copy-start.2 = (bf16[4,8,8,1536]{3,2,1,0:T(8,128)(2,1)S(1)}, bf16[4,8,8,1536]{3,2,1,0:T(8,128)(2,1)}, u32[]{:S(2)}) copy-start(bf16[4,8,8,1536]{3,2,1,0:T(8,128)(2,1)} %pad_maximum_fusion.1) | copy-start | bytes 2359300
  195.0 1.1 copy-start.6
  196.1 1.1 copy-start.9
  197.3 1.1 copy-start.8
  198.4 1.1 copy-start.7
  199.5 1.1 copy-start.5
  200.7 1.1 copy-start.4
  201.8 1.1 copy-start.3
  202.4 2.0 copy-start.1
  (6 other events, 4.8 us)
Sparse Core Ops, SparseCore 0:
  8.9 174.3 all-gather.2
